TPU v7x, 32 devices: a whole 2x2x4 slice. The times are simulated.
32 devices in a mesh: groups: 2 (over x), dev: 8 (over z, y), rve: 2 (over core).
Axes of the slice: x: 2, y: 2, z: 4, core: 2. Of those that a mesh axis runs over, the one named last changes fastest.
Arguments:
- phase: int32 [4, 64, 128, 128], P(('groups', 'rve'), 'dev'), parts along dimension 0, may hold values from 0 to 2
- load_case: int32 [4], P(('groups', 'rve')), parts along dimension 0, may hold values from 0 to 5
- moduli: float32 [2, 3], replicated, may hold values from 0.5 to 8
- loading_table: float32 [6, 3, 3], replicated, may hold values from -4 to 4
- w_embed: bfloat16 [1408, 768], P(('dev', 'rve')), may hold values from -0.21875 to 0.21875
- w_up: bfloat16 [3072, 1408], P(('dev', 'rve')), may hold values from -0.15625 to 0.15625
- cotangent: bfloat16 [16384, 3072], P(('groups', 'dev', 'rve')), parts along dimension 0, may hold values from -6 to 6
Outputs:
- displacement: float32 [4, 3, 64, 128, 128], P(('groups', 'rve'), None, 'dev'), parts along dimension 0
- grad_embed: float32 [2816, 768], P(('groups', 'dev', 'rve')), parts along dimension 0
- grad_up: float32 [6144, 1408], P(('groups', 'dev', 'rve')), parts along dimension 0
There are 2 independent parts, one for each index of `groups`. A program takes and returns all parts, laid end to end along the dimension named above; an argument that names none is the same for every part. Nothing has to cross between parts.
Inputs may be any that keep to these rules, and one draw needn't show every extreme that they name: `load_case`: row of loading_table for each RVE.
All inputs are finite; a program needn't handle non-finite values.
Results may differ from a plain program's by a relative error of at most 0.0069.
Values may be sent and summed in bfloat16 or wider, within the bound.
No kernel may reach another device: no remote copies, remote signals or barrier semaphores. Data moves between devices by JAX's collectives and lax.ppermute only.
A program may use at most 128 MiB of HBM per device.

v0:
```python
from functools import partial
import math
import jax
import jax.numpy as jnp
from jax import lax
from jax.sharding import PartitionSpec as P

PATCH_X = 8
PATCH_Y = 8
PATCH_Z = 4
SWEEPS = 4
epsilon = 1e-06


def with_halo(value, sides, width):
    for axis, dim in sides:
        size, length = (lax.axis_size(axis), value.shape[dim])
        up = [(i, (i + 1) % size) for i in range(size - 1)]
        down = [(j, i) for i, j in up]
        last = lax.slice_in_dim(value, length - width, length, axis=dim)
        initial = lax.slice_in_dim(value, 0, width, axis=dim)
        before = lax.ppermute(last, axis, up)
        after = lax.ppermute(initial, axis, down)
        value = jnp.concatenate([before, value, after], axis=dim)
    return value


def stiffness(phase, moduli):
    labels = jnp.arange(moduli.shape[1], dtype=jnp.int32)
    member = (labels[:, None, None, None] == phase[None]).astype(jnp.float32)
    shear_stiff = jnp.sum(member * moduli[0][:, None, None, None], axis=0)
    axial_stiff = jnp.sum(member * moduli[1][:, None, None, None], axis=0)
    return (shear_stiff, axial_stiff)


def harmonic(here, there, in_here, in_there):
    blended = 2.0 * here * there / (here + there)
    return jnp.where(in_here & in_there, blended, jnp.where(in_here, here, there))


def face_pairs(stiff, inside):
    stiff = jnp.where(inside, stiff, 1.0)
    padded = jnp.pad(stiff, 1, constant_values=1.0)
    in_pad = jnp.pad(inside, 1)
    face_list = []
    for direction in range(3):
        upper_cut = [slice(1, -1)] * 3
        lower_cut = [slice(1, -1)] * 3
        upper_cut[direction] = slice(2, None)
        lower_cut[direction] = slice(0, -2)
        upper_face = harmonic(stiff, padded[tuple(upper_cut)], inside, in_pad[tuple(upper_cut)])
        lower_face = harmonic(stiff, padded[tuple(lower_cut)], inside, in_pad[tuple(lower_cut)])
        face_list.append((upper_face, lower_face))
    return face_list


def operator_terms(shear_stiff, axial_stiff, inside, strain):
    shear_faces = face_pairs(shear_stiff, inside)
    axial_faces = face_pairs(axial_stiff, inside)
    terms = []
    for component in range(3):
        face_list = [
            axial_faces[direction] if direction == component else shear_faces[direction]
            for direction in range(3)
        ]
        forcing = strain[component, 0] * (face_list[0][0] - face_list[0][1])
        diagonal = face_list[0][0] + face_list[0][1]
        for direction in (1, 2):
            forcing = forcing + strain[component, direction] * (
                face_list[direction][0] - face_list[direction][1]
            )
            diagonal = diagonal + face_list[direction][0] + face_list[direction][1]
        terms.append((face_list, forcing, diagonal))
    return terms


def first_iterate(terms, inside):
    return jnp.stack(
        [jnp.where(inside, forcing / diagonal, 0.0) for face_list, forcing, diagonal in terms]
    )


def jacobi_sweep(ghosted, terms, inside):
    results = []
    for component in range(3):
        face_list, forcing, diagonal = terms[component]
        padded = jnp.pad(ghosted[component], ((0, 0), (1, 1), (1, 1)))
        summed = forcing
        for direction in range(3):
            upper_cut = [slice(1, -1)] * 3
            lower_cut = [slice(1, -1)] * 3
            upper_cut[direction] = slice(2, None)
            lower_cut[direction] = slice(0, -2)
            summed = (
                summed
                + face_list[direction][0] * padded[tuple(upper_cut)]
                + face_list[direction][1] * padded[tuple(lower_cut)]
            )
        results.append(jnp.where(inside, summed / diagonal, 0.0))
    return jnp.stack(results)


def row_mask(first_global, row_total, grid_rows, plane_shape):
    global_rows = first_global + jnp.arange(row_total, dtype=jnp.int32)
    within = (global_rows >= 0) & (global_rows < grid_rows)
    return jnp.broadcast_to(within[:, None, None], (row_total,) + tuple(plane_shape))


def contract_last(left, right):
    return lax.dot_general(
        left, right, (((1,), (1,)), ((), ())), preferred_element_type=jnp.float32
    )


def contract_first(left, right):
    return lax.dot_general(
        left, right, (((0,), (0,)), ((), ())), preferred_element_type=jnp.float32
    )


def gelu_grad(pre_act, cotangent):
    _, pullback = jax.vjp(partial(jax.nn.gelu, approximate=True), pre_act)
    return pullback(cotangent.astype(jnp.float32))[0].astype(jnp.bfloat16)


def local(phase, load_case, moduli, loading_table, w_embed, w_up, cotangent):
    local_phase = phase[0]
    slab_rows = local_phase.shape[0]
    plane_shape = local_phase.shape[1:]
    dev_count = lax.axis_size("dev")
    rve_count = lax.axis_size("rve")
    first_row = lax.axis_index("dev") * slab_rows
    grid_rows = slab_rows * dev_count
    shear_stiff, axial_stiff = stiffness(local_phase, moduli)
    case_labels = jnp.arange(loading_table.shape[0], dtype=jnp.int32)
    case_pick = (case_labels == load_case[0]).astype(jnp.float32)
    strain = jnp.sum(case_pick[:, None, None] * loading_table, axis=0)
    stacked = jnp.stack([shear_stiff, axial_stiff])
    ghosted = with_halo(stacked, (("dev", 1),), SWEEPS)
    inside = row_mask(first_row - SWEEPS, slab_rows + 2 * SWEEPS, grid_rows, plane_shape)
    terms = operator_terms(ghosted[0], ghosted[1], inside, strain)
    displace = first_iterate(terms, inside)
    for repeat in range(SWEEPS - 1):
        displace = jacobi_sweep(jnp.pad(displace, ((0, 0), (1, 1), (0, 0), (0, 0))), terms, inside)
    displace = displace[:, SWEEPS : SWEEPS + slab_rows]
    rounded = displace.astype(jnp.bfloat16)
    ny_cells = rounded.shape[2]
    nz_cells = rounded.shape[3]
    band_rows = ny_cells // dev_count
    blocks = rounded.reshape(3, slab_rows, dev_count, band_rows, nz_cells)
    regrouped = lax.all_to_all(blocks, "dev", split_axis=2, concat_axis=1, tiled=True)
    grid_x = regrouped.shape[1]
    cells = regrouped.reshape(
        3, grid_x // PATCH_X, PATCH_X, band_rows // PATCH_Y, PATCH_Y, nz_cells // PATCH_Z, PATCH_Z
    )
    patches = cells.transpose(3, 1, 5, 0, 2, 4, 6).reshape(-1, 3 * PATCH_X * PATCH_Y * PATCH_Z)
    token_count = patches.shape[0]
    grad_scale = 1.0 / math.sqrt(token_count * dev_count * rve_count)
    embedded = contract_last(
        patches, lax.all_gather(w_embed, ("dev", "rve"), axis=0, tiled=True)
    ).astype(jnp.bfloat16)
    embed_wide = embedded.astype(jnp.float32)
    inverse_rms = lax.rsqrt(jnp.mean(embed_wide * embed_wide, axis=-1, keepdims=True) + epsilon)
    normed_wide = embed_wide * inverse_rms
    normed = normed_wide.astype(jnp.bfloat16)
    up_all = lax.all_gather(w_up, ("dev", "rve"), axis=0, tiled=True)
    pre_act = contract_last(normed, up_all)
    act_grad = gelu_grad(pre_act, cotangent)
    columns = act_grad
    grad_up = (
        lax.psum_scatter(
            contract_first(columns, normed), ("dev", "rve"), scatter_dimension=0, tiled=True
        )
        * grad_scale
    )
    normed_grad = jnp.dot(act_grad, up_all, preferred_element_type=jnp.float32)
    embed_in_grad = (
        inverse_rms
        * (normed_grad - normed_wide * jnp.mean(normed_grad * normed_wide, axis=-1, keepdims=True))
    ).astype(jnp.bfloat16)
    columns = embed_in_grad
    grad_embed = (
        lax.psum_scatter(
            contract_first(columns, patches), ("dev", "rve"), scatter_dimension=0, tiled=True
        )
        * grad_scale
    )
    return (displace[None], grad_embed, grad_up)


def solution(mesh):
    return jax.shard_map(
        local,
        mesh=mesh,
        in_specs=(
            P(("groups", "rve"), "dev", None, None),
            P(("groups", "rve")),
            P(),
            P(),
            P(("dev", "rve"), None),
            P(("dev", "rve"), None),
            P(("groups", "dev", "rve"), None),
        ),
        out_specs=(
            P(("groups", "rve"), None, "dev", None, None),
            P(("groups", "dev", "rve"), None),
            P(("groups", "dev", "rve"), None),
        ),
        check_vma=False,
    )
```

profile of v0, /device:TPU:0, one launch (start us, length us, event | category | flops | bytes accessed | tf_op | source)
XLA Modules:
  0.0 482.8 jit_solution(5209808814416989539)
XLA Ops:
  7.2 0.7 all-gather.3.cloned.1.call-update
  8.0 0.7 all-gather.5.cloned.1.call-update
  8.7 0.8 slice_bitcast_fusion.29
  9.5 1.5 select_reduce_fusion.1
  11.1 1.3 collective-permute-start.1
  12.4 5.6 %collective-permute-start = (f32[2,4,128,128]{3,2,1,0:T(8,128)S(1)}, f32[2,4,128,128]{3,2,1,0:T(8,128)S(1)}, u32[]{:S(2)}, u32[]{:S(2)}) collective-permute-start(f32[2,4,128,128]{3,2,1,0:T(8,128)S(1)} %get-tuple-element.31), channel_id=1, source_target_pairs={{0,2},{2,4},{4,6},{6,8},{8,10},{10,12},{12,14},{1,3},{3,5},{5,7},{... | collective-permute-start | bytes 1572872 | tf_op jit(solution)/shard_map/ppermute | solution.py:22
  18.7 0.7 fusion.159
  19.4 10.0 %collective-permute-done.1 = f32[2,4,128,128]{3,2,1,0:T(8,128)S(1)} collective-permute-done((f32[2,4,128,128]{3,2,1,0:T(8,128)S(1)}, f32[2,4,128,128]{3,2,1,0:T(8,128)S(1)}, u32[]{:S(2)}, u32[]{:S(2)}) %collective-permute-start.1) | collective-permute-done | bytes 524320 | tf_op jit(solution)/shard_map/ppermute | solution.py:23
  29.3 11.4 %collective-permute-done = f32[2,4,128,128]{3,2,1,0:T(8,128)S(1)} collective-permute-done((f32[2,4,128,128]{3,2,1,0:T(8,128)S(1)}, f32[2,4,128,128]{3,2,1,0:T(8,128)S(1)}, u32[]{:S(2)}, u32[]{:S(2)}) %collective-permute-start) | collective-permute-done | bytes 524320 | tf_op jit(solution)/shard_map/ppermute | solution.py:22
  40.9 0.3 fusion.140
  41.1 0.1 broadcast_in_dim.32
  41.3 5.2 %select_bitcast_fusion.11 = (f32[1,16,128,128]{3,2,1,0:T(8,128)S(1)}, f32[16,128,128]{2,1,0:T(8,128)S(1)}, f32[16,128,128]{2,1,0:T(8,128)S(1)}, f32[16,128,128]{...) fusion(f32[]{:T(128)} %bitcast.10, f32[]{:T(128)} %bitcast.8, ...), kind=kLoop, calls=%fused_computation.274 | loop fusion | flops 13893632 | bytes 9699356 | tf_op jit(solution)/shard_map/stack | solution.py:78
  46.5 4.3 select_bitcast_fusion.10
  50.8 3.5 select_bitcast_fusion.9
  54.2 0.5 select_maximum_fusion.4
  54.7 0.4 slice_bitcast_fusion.8
  55.1 3.5 select_bitcast_fusion.6
  58.6 3.3 select_bitcast_fusion.7
  61.9 3.3 select_bitcast_fusion.8
  65.2 0.5 select_maximum_fusion.2
  65.7 0.4 slice_bitcast_fusion.5
  66.1 3.5 select_bitcast_fusion.3
  69.6 3.3 select_bitcast_fusion.4
  72.9 3.3 select_bitcast_fusion.5
  76.2 0.5 select_maximum_fusion
  76.7 0.4 slice_bitcast_fusion.2
  77.1 3.5 select_bitcast_fusion
  80.6 3.3 select_bitcast_fusion.1
  83.9 3.3 select_bitcast_fusion.2
  87.4 0.2 copy.17
  87.7 42.7 %all_to_all.15 = bf16[3,8,8,16,128]{4,3,1,0,2:T(8,128)(2,1)S(1)} all-to-all(bf16[3,8,8,16,128]{4,3,1,0,2:T(8,128)(2,1)S(1)} %copy.17), channel_id=1, replica_groups=mesh['groups'=2,'dev'=8,'rve'=2] {'dev'}, dimensions={2} | all-to-all | bytes 1572864 | tf_op jit(solution)/shard_map/all_to_all | solution.py:151
  130.4 4.5 copy.18
  134.9 21.6 %reshape.61 = bf16[3,8,8,2,8,32,4]{4,3,6,5,2,1,0:T(2,128)(2,1)} reshape(bf16[3,8,8,1,16,128]{4,5,2,1,0,3:T(8,128)(2,1)} %copy.18) | data formatting | bytes 1572864 | tf_op jit(solution)/shard_map/reshape | solution.py:153
  156.5 29.5 %copy.19 = bf16[2,8,32,3,8,8,4]{2,1,0,6,5,4,3:T(8,128)(2,1)S(1)} copy(bf16[2,8,32,3,8,8,4]{5,0,6,2,4,1,3:T(2,128)(2,1)} %bitcast.270) | data formatting | bytes 1572864 | tf_op jit(solution)/shard_map/transpose | solution.py:156
  186.0 3.8 reshape.62
  189.8 3.4 fusion.18
  193.2 12.2 %fusion.2 = bf16[512,3072]{1,0:T(8,128)(2,1)S(1)} fusion(bf16[512,3072]{1,0:T(8,128)(2,1)} %param.13, bf16[3072,1408]{1,0:T(8,128)(2,1)} %all-gather.5.cloned.1.call-done, bf16[512,1408]{1,0:T(8,128)(2,1)S(1)} %get-tuple-element.45, f32[512]{0:T(512)S(1)} %add_rsqrt_fusion), kind=kOutput, calls=%fused_computation.6 | convolution fusion | flops 4464377856 | bytes 16386048 | tf_op jit(solution)/shard_map/dot_general | solution.py:110
  205.5 5.1 %fusion.14 = (f32[512]{0:T(512)S(1)}, f32[512,1408]{1,0:T(8,128)S(1)}) fusion(bf16[512,1408]{1,0:T(8,128)(2,1)S(1)} %get-tuple-element.45, f32[512]{0:T(512)S(1)} %add_rsqrt_fusion, bf16[512,3072]{1,0:T(8,128)(2,1)S(1)} %fusion.2, bf16[3072,1408]{1,0:T(8,128)(2,1)S(1)} %copy-done.8), kind=kOutput, calls=%fused_computation.83 | convolution fusion | flops 4432068096 | bytes 16125952 | tf_op jit(solution)/shard_map/dot_general | solution.py:176
  210.6 3.7 fusion.19
  214.4 11.0 %fusion.150 = f32[3072,1408]{1,0:T(8,128)} fusion(bf16[512,3072]{1,0:T(8,128)(2,1)} %copy-done.9, bf16[512,1408]{1,0:T(8,128)(2,1)S(1)} %get-tuple-element.45, f32[512]{0:T(512)S(1)} %add_rsqrt_fusion), kind=kOutput, calls=%fused_computation.289 | convolution fusion | flops 4431347712 | bytes 21891072 | tf_op jit(solution)/shard_map/dot_general | solution.py:116
  225.4 1.3 copy-done.1
  226.7 0.4 copy-done.3
  227.0 0.4 copy-done.5
  227.4 1.2 fusion.157
  228.7 60.2 %reduce-scatter.3.cloned.1.call-done = f32[88,768]{1,0:T(8,128)} async-done(((f32[1408,768]{1,0:T(8,128)}), f32[88,768]{1,0:T(8,128)}) %reduce-scatter.3.cloned.1.call-update) | async-done | bytes 270352 | tf_op jit(solution)/shard_map/reduce_scatter | solution.py:183
  288.9 1.7 broadcast_multiply_fusion.1
  290.6 183.4 %reduce-scatter.5.cloned.1.call-done = f32[192,1408]{1,0:T(8,128)} async-done(((f32[3072,1408]{1,0:T(8,128)}), f32[192,1408]{1,0:T(8,128)}) %reduce-scatter.5.cloned.1.call-update) | async-done | bytes 1081360 | tf_op jit(solution)/shard_map/reduce_scatter | solution.py:171
  474.0 2.3 broadcast_multiply_fusion
  (33 shorter events, 0.7 us)
Async XLA Ops:
  7.2 11.4 %copy-start.7 = (f32[6,3,3]{0,2,1:T(4,128)S(1)}, f32[6,3,3]{0,2,1:T(4,128)}, u32[]{:S(2)}) copy-start(f32[6,3,3]{0,2,1:T(4,128)} %param.10) | copy-start | bytes 652
  7.2 182.6 %all-gather.3.cloned.1.call-start = ((), (), s32[]{:S(2)}) async-start(), calls=%async_computation.3 | async-start | bytes 2297856 | tf_op jit(solution)/shard_map/all_gather | solution.py:160
  7.9 185.3 %all-gather.5.cloned.1.call-start = ((), (), s32[]{:S(2)}) async-start(), calls=%async_computation.4 | async-start | bytes 9191424 | tf_op jit(solution)/shard_map/all_gather | solution.py:166
  8.7 280.3 %reduce-scatter.3.cloned.1.call-start = ((), (), s32[]{:S(2)}) async-start(), calls=%async_computation.5 | async-start | bytes 4595712 | tf_op jit(solution)/shard_map/reduce_scatter | solution.py:183
  11.1 18.3 %collective-permute-start.1 = (f32[2,4,128,128]{3,2,1,0:T(8,128)S(1)}, f32[2,4,128,128]{3,2,1,0:T(8,128)S(1)}, u32[]{:S(2)}, u32[]{:S(2)}) collective-permute-start(f32[2,4,128,128]{3,2,1,0:T(8,128)S(1)} %get-tuple-element.32), channel_id=1, source_target_pairs={{2,0},{4,2},{6,4},{8,6},{10,8},{12,10},{14,12},{3,1},{5,3},{7,5},{... | collective-permute-start | bytes 1572872 | tf_op jit(solution)/shard_map/ppermute | solution.py:23
  12.4 28.4 %collective-permute-start = (f32[2,4,128,128]{3,2,1,0:T(8,128)S(1)}, f32[2,4,128,128]{3,2,1,0:T(8,128)S(1)}, u32[]{:S(2)}, u32[]{:S(2)}) collective-permute-start(f32[2,4,128,128]{3,2,1,0:T(8,128)S(1)} %get-tuple-element.31), channel_id=1, source_target_pairs={{0,2},{2,4},{4,6},{6,8},{8,10},{10,12},{12,14},{1,3},{3,5},{5,7},{... | collective-permute-start | bytes 1572872 | tf_op jit(solution)/shard_map/ppermute | solution.py:22
  80.6 6.7 %copy-start = (f32[1,16,128,128]{3,2,1,0:T(8,128)}, f32[1,16,128,128]{3,2,1,0:T(8,128)S(1)}, u32[]{:S(2)}) copy-start(f32[1,16,128,128]{3,2,1,0:T(8,128)S(1)} %select_bitcast_fusion) | copy-start | bytes 3145732
  83.9 3.4 copy-start.2
  87.3 43.1 %copy-start.4 = (f32[1,16,128,128]{3,2,1,0:T(8,128)}, f32[1,16,128,128]{3,2,1,0:T(8,128)S(1)}, u32[]{:S(2)}) copy-start(f32[1,16,128,128]{3,2,1,0:T(8,128)S(1)} %select_bitcast_fusion.2) | copy-start | bytes 3145732
  193.2 12.2 %copy-start.8 = (bf16[3072,1408]{1,0:T(8,128)(2,1)S(1)}, bf16[3072,1408]{1,0:T(8,128)(2,1)}, u32[]{:S(2)}) copy-start(bf16[3072,1408]{1,0:T(8,128)(2,1)} %all-gather.5.cloned.1.call-done) | copy-start | bytes 25952260
  205.5 5.1 %copy-start.9 = (bf16[512,3072]{1,0:T(8,128)(2,1)}, bf16[512,3072]{1,0:T(8,128)(2,1)S(1)}, u32[]{:S(2)}) copy-start(bf16[512,3072]{1,0:T(8,128)(2,1)S(1)} %fusion.2) | copy-start | bytes 9437188
  205.5 5.1 %copy-start.6 = (bf16[512,768]{0,1:T(8,128)(2,1)S(1)}, bf16[512,768]{0,1:T(8,128)(2,1)}, u32[]{:S(2)}) copy-start(bf16[512,768]{0,1:T(8,128)(2,1)} %reshape.62) | copy-start | bytes 2359300
  214.3 259.6 %reduce-scatter.5.cloned.1.call-start = ((), (), s32[]{:S(2)}) async-start(), calls=%async_computation.6 | async-start | bytes 18382848 | tf_op jit(solution)/shard_map/reduce_scatter | solution.py:171
  225.4 1.3 copy-start.1
  225.4 1.7 copy-start.3
  225.4 2.0 copy-start.5
Sparse Core Ops, SparseCore 0:
  10.2 54.4 all-gather.2
  67.0 83.2 all-gather.4
  214.5 74.4 reduce-scatter.2
  292.9 181.0 reduce-scatter.4
where the time goes:
time: 485 us; the launch traced here: 483 us
  waiting for transfers between devices  266 us (55%)
  local copies, waits for them, and re-layouts  64.5 us (13%)
  other arithmetic  52.1 us (11%)
  blocking collectives  42.7 us (9%)
  matrix products  35.4 us (7%)
  between operations  14.8 us (3%)
  starting transfers between devices  7.01 us (1%)
    reduce_scatter x1, waiting for transfers between devices, local(): lax.psum_scatter(contract_first(columns, normed), ('dev', 'rve'), scatter...  183 us
    reduce_scatter x1, waiting for transfers between devices, local(): lax.psum_scatter(contract_first(columns, patches), ('dev', 'rve'), scatte...  60.2 us
    all_to_all x1, blocking collectives, local(): lax.all_to_all(blocks, 'dev', split_axis=2, concat_axis=1, tiled=True)  42.7 us
    another operation x11, other arithmetic, jacobi_sweep(): return jnp.stack(results)  31.2 us
    transpose x1, local copies, waits for them, and re-layouts, local(): cells.transpose(3, 1, 5, 0, 2, 4, 6)  29.5 us
    reshape x1, local copies, waits for them, and re-layouts, local(): regrouped.reshape(3, grid_x // PATCH_X, PATCH_X, band_rows // PATCH_Y, PA...  21.6 us
    dot_general x2, matrix products, contract_last(): lax.dot_general(left, right, (((1,), (1,)), ((), ())), preferred_element_...  15.6 us
    dot_general x2, matrix products, contract_first(): lax.dot_general(left, right, (((0,), (0,)), ((), ())), preferred_element_...  14.7 us
  transfers between devices with their start and end apart: 6, of which 4 were waited for; matrix products, arithmetic and copies ran while one was open for 26% of the time, Pallas kernels for 0%

commit v1 on v0

--- a/solution.py
+++ b/solution.py
@@ -10,6 +10,18 @@
 PATCH_Z = 4
 SWEEPS = 4
 epsilon = 1e-06
+
+
+def sent_to_each(x, axis, split, join):
+    ways, here = (lax.axis_size(axis), lax.axis_index(axis))
+    width = x.shape[split] // ways
+    turned = jnp.roll(x, -here * width, axis=split)
+    got = [lax.slice_in_dim(turned, 0, width, axis=split)]
+    for far in range(1, ways):
+        sent = lax.slice_in_dim(turned, far * width, (far + 1) * width, axis=split)
+        got.append(lax.ppermute(sent, axis, [(d, (d + far) % ways) for d in range(ways)]))
+    line = jnp.concatenate(got[::-1], axis=join)
+    return jnp.roll(line, (here + 1) * got[0].shape[join], axis=join)
 
 
 def with_halo(value, sides, width):
@@ -148,7 +160,7 @@
     nz_cells = rounded.shape[3]
     band_rows = ny_cells // dev_count
     blocks = rounded.reshape(3, slab_rows, dev_count, band_rows, nz_cells)
-    regrouped = lax.all_to_all(blocks, "dev", split_axis=2, concat_axis=1, tiled=True)
+    regrouped = sent_to_each(blocks, "dev", 2, 1)
     grid_x = regrouped.shape[1]
     cells = regrouped.reshape(
         3, grid_x // PATCH_X, PATCH_X, band_rows // PATCH_Y, PATCH_Y, nz_cells // PATCH_Z, PATCH_Z

time: 485 us -> 458 us (0.944)
  blocking collectives: 42.7 us -> 0 us
  waiting for transfers between devices: 266 us -> 298 us
  local copies, waits for them, and re-layouts: 64.5 us -> 37.7 us
  starting transfers between devices: 7.01 us -> 18.1 us
    all_to_all x1 -> x0, blocking collectives: 42.7 us -> none  [local(): lax.all_to_all(blocks, 'dev', split_axis=2, concat_axis=1, tiled=True)]
    ppermute x0 -> x7, waiting for transfers between devices: none -> 25.3 us  [sent_to_each(): lax.ppermute(sent, axis, [(d, (d + far) % ways) for d in range(ways)])]
    transpose x1, local copies, waits for them, and re-layouts: 29.5 us -> 16.4 us  [local(): cells.transpose(3, 1, 5, 0, 2, 4, 6)]
    ppermute x0 -> x7, starting transfers between devices: none -> 11.1 us  [sent_to_each(): lax.ppermute(sent, axis, [(d, (d + far) % ways) for d in range(ways)])]
    reshape x1, local copies, waits for them, and re-layouts: 21.6 us -> 10.7 us  [local(): regrouped.reshape(3, grid_x // PATCH_X, PATCH_X, band_rows // PATCH_Y, PA...]
    reduce_scatter x1, waiting for transfers between devices: 60.2 us -> 67 us  [local(): lax.psum_scatter(contract_first(columns, patches), ('dev', 'rve'), scatte...]
  transfers between devices with their start and end apart: 6 -> 13, of which waited for: 4 -> 7; matrix products, arithmetic and copies ran while one was open for 26% -> 22% of each run, Pallas kernels for 0% -> 0%
where the time goes in v1:
time: 458 us; the launch traced here: 457 us
  waiting for transfers between devices  298 us (65%)
  other arithmetic  53.3 us (12%)
  local copies, waits for them, and re-layouts  37.7 us (8%)
  matrix products  35.1 us (8%)
  starting transfers between devices  18.1 us (4%)
  between operations  14.9 us (3%)
    reduce_scatter x1, waiting for transfers between devices, local(): lax.psum_scatter(contract_first(columns, normed), ('dev', 'rve'), scatter...  183 us
    reduce_scatter x1, waiting for transfers between devices, local(): lax.psum_scatter(contract_first(columns, patches), ('dev', 'rve'), scatte...  67 us
    another operation x11, other arithmetic, jacobi_sweep(): return jnp.stack(results)  31.9 us
    ppermute x7, waiting for transfers between devices, sent_to_each(): lax.ppermute(sent, axis, [(d, (d + far) % ways) for d in range(ways)])  25.3 us
    transpose x1, local copies, waits for them, and re-layouts, local(): cells.transpose(3, 1, 5, 0, 2, 4, 6)  16.4 us
    dot_general x2, matrix products, contract_last(): lax.dot_general(left, right, (((1,), (1,)), ((), ())), preferred_element_...  15.6 us
    dot_general x2, matrix products, contract_first(): lax.dot_general(left, right, (((0,), (0,)), ((), ())), preferred_element_...  14.3 us
    another operation x4, other arithmetic, first_iterate(): jnp.stack([jnp.where(inside, forcing / diagonal, 0.0) for face_list, forc...  13.6 us
  transfers between devices with their start and end apart: 13, of which 7 were waited for; matrix products, arithmetic and copies ran while one was open for 22% of the time, Pallas kernels for 0%

profile of v1, /device:TPU:0, one launch (start us, length us, event | category | flops | bytes accessed | tf_op | source)
XLA Modules:
  0.0 457.4 jit_solution(13875140030518863803)
XLA Ops:
  7.2 0.7 all-gather.3.cloned.1.call-update
  8.0 0.7 all-gather.5.cloned.1.call-update
  8.7 0.8 slice_bitcast_fusion.29
  9.5 1.5 select_reduce_fusion.1
  11.1 1.3 collective-permute-start.1
  12.4 5.6 %collective-permute-start = (f32[2,4,128,128]{3,2,1,0:T(8,128)S(1)}, f32[2,4,128,128]{3,2,1,0:T(8,128)S(1)}, u32[]{:S(2)}, u32[]{:S(2)}) collective-permute-start(f32[2,4,128,128]{3,2,1,0:T(8,128)S(1)} %get-tuple-element.31), channel_id=1, source_target_pairs={{0,2},{2,4},{4,6},{6,8},{8,10},{10,12},{12,14},{1,3},{3,5},{5,7},{... | collective-permute-start | bytes 1572872 | tf_op jit(solution)/shard_map/ppermute | solution.py:34
  18.7 0.7 fusion.161
  19.4 9.9 %collective-permute-done.1 = f32[2,4,128,128]{3,2,1,0:T(8,128)S(1)} collective-permute-done((f32[2,4,128,128]{3,2,1,0:T(8,128)S(1)}, f32[2,4,128,128]{3,2,1,0:T(8,128)S(1)}, u32[]{:S(2)}, u32[]{:S(2)}) %collective-permute-start.1) | collective-permute-done | bytes 524320 | tf_op jit(solution)/shard_map/ppermute | solution.py:35
  29.3 11.4 %collective-permute-done = f32[2,4,128,128]{3,2,1,0:T(8,128)S(1)} collective-permute-done((f32[2,4,128,128]{3,2,1,0:T(8,128)S(1)}, f32[2,4,128,128]{3,2,1,0:T(8,128)S(1)}, u32[]{:S(2)}, u32[]{:S(2)}) %collective-permute-start) | collective-permute-done | bytes 524320 | tf_op jit(solution)/shard_map/ppermute | solution.py:34
  41.3 5.3 %select_bitcast_fusion.11 = (f32[1,16,128,128]{3,2,1,0:T(8,128)S(1)}, f32[16,128,128]{2,1,0:T(8,128)S(1)}, f32[16,128,128]{2,1,0:T(8,128)S(1)}, f32[16,128,128]{...) fusion(f32[]{:T(128)} %bitcast.10, f32[]{:T(128)} %bitcast.8, ...), kind=kLoop, calls=%fused_computation.276 | loop fusion | flops 13893632 | bytes 9699356 | tf_op jit(solution)/shard_map/stack | solution.py:90
  46.6 4.4 select_bitcast_fusion.10
  51.0 3.5 select_bitcast_fusion.9
  54.5 0.5 select_maximum_fusion.4
  55.4 3.5 select_bitcast_fusion.6
  58.8 3.4 select_bitcast_fusion.7
  62.2 3.5 select_bitcast_fusion.8
  65.7 0.5 select_maximum_fusion.2
  66.6 3.5 select_bitcast_fusion.3
  70.0 3.4 select_bitcast_fusion.4
  73.4 3.5 select_bitcast_fusion.5
  76.9 0.5 select_maximum_fusion
  77.8 3.5 select_bitcast_fusion
  81.3 3.4 select_bitcast_fusion.1
  84.7 3.5 select_bitcast_fusion.2
  88.6 0.6 copy-done.4
  89.4 2.7 collective-permute-start.2
  92.1 3.3 collective-permute-start.3
  95.4 2.1 collective-permute-start.5
  97.5 0.8 collective-permute-start.6
  98.4 1.9 collective-permute-start.7
  100.6 1.3 collective-permute-done.4
  101.8 23.2 %collective-permute-done.5 = bf16[3,8,1,16,128]{4,3,2,1,0:T(8,128)(2,1)S(1)} collective-permute-done((bf16[3,8,1,16,128]{4,3,2,1,0:T(8,128)(2,1)S(1)}, bf16[3,8,1,16,128]{4,3,2,1,0:T(8,128)(2,1)S(1)}, u32[]{:S(2)}, u32[]{:S(2)}) %collective-permute-start.5) | collective-permute-done | bytes 98336 | tf_op jit(solution)/shard_map/ppermute | solution.py:22
  125.0 0.8 collective-permute-done.6
  126.3 0.9 copy.15
  127.3 10.7 %reshape.60 = bf16[3,8,8,2,8,32,4]{2,1,6,5,4,3,0:T(8,128)(2,1)} reshape(bf16[3,64,1,16,128]{1,4,3,0,2:T(8,128)(2,1)S(1)} %copy.15) | data formatting | bytes 1572864 | tf_op jit(solution)/shard_map/reshape | solution.py:165
  138.0 16.4 %copy.16 = bf16[2,8,32,3,8,8,4]{2,1,0,6,5,4,3:T(8,128)(2,1)S(1)} copy(bf16[2,8,32,3,8,8,4]{4,1,6,2,5,0,3:T(8,128)(2,1)} %bitcast.267) | data formatting | bytes 1572864 | tf_op jit(solution)/shard_map/transpose | solution.py:168
  154.4 3.8 reshape.61
  158.1 3.4 fusion.18
  161.6 12.2 %fusion.2 = bf16[512,3072]{1,0:T(8,128)(2,1)S(1)} fusion(bf16[512,3072]{1,0:T(8,128)(2,1)} %param.13, bf16[3072,1408]{1,0:T(8,128)(2,1)} %all-gather.5.cloned.1.call-done, bf16[512,1408]{1,0:T(8,128)(2,1)S(1)} %get-tuple-element.52, f32[512]{0:T(512)S(1)} %add_rsqrt_fusion), kind=kOutput, calls=%fused_computation.6 | convolution fusion | flops 4464377856 | bytes 16386048 | tf_op jit(solution)/shard_map/dot_general | solution.py:122
  173.9 5.1 %fusion.14 = (f32[512]{0:T(512)S(1)}, f32[512,1408]{1,0:T(8,128)S(1)}) fusion(bf16[512,1408]{1,0:T(8,128)(2,1)S(1)} %get-tuple-element.52, f32[512]{0:T(512)S(1)} %add_rsqrt_fusion, bf16[512,3072]{1,0:T(8,128)(2,1)S(1)} %fusion.2, bf16[3072,1408]{1,0:T(8,128)(2,1)S(1)} %copy-done.8), kind=kOutput, calls=%fused_computation.83 | convolution fusion | flops 4432068096 | bytes 16125952 | tf_op jit(solution)/shard_map/dot_general | solution.py:188
  179.0 3.7 fusion.19
  182.8 10.6 %fusion.151 = f32[3072,1408]{1,0:T(8,128)} fusion(bf16[512,3072]{1,0:T(8,128)(2,1)} %copy-done.9, bf16[512,1408]{1,0:T(8,128)(2,1)S(1)} %get-tuple-element.52, f32[512]{0:T(512)S(1)} %add_rsqrt_fusion), kind=kOutput, calls=%fused_computation.292 | convolution fusion | flops 4431347712 | bytes 21891072 | tf_op jit(solution)/shard_map/dot_general | solution.py:128
  193.4 1.2 copy-done.1
  195.3 1.2 fusion.158
  196.6 67.0 %reduce-scatter.3.cloned.1.call-done = f32[88,768]{1,0:T(8,128)} async-done(((f32[1408,768]{1,0:T(8,128)}), f32[88,768]{1,0:T(8,128)}) %reduce-scatter.3.cloned.1.call-update) | async-done | bytes 270352 | tf_op jit(solution)/shard_map/reduce_scatter | solution.py:195
  263.5 1.7 broadcast_multiply_fusion.1
  265.2 183.3 %reduce-scatter.5.cloned.1.call-done = f32[192,1408]{1,0:T(8,128)} async-done(((f32[3072,1408]{1,0:T(8,128)}), f32[192,1408]{1,0:T(8,128)}) %reduce-scatter.5.cloned.1.call-update) | async-done | bytes 1081360 | tf_op jit(solution)/shard_map/reduce_scatter | solution.py:183
  448.5 2.3 broadcast_multiply_fusion
  (64 shorter events, 4.1 us)
Async XLA Ops:
  7.2 11.5 %copy-start.7 = (f32[6,3,3]{0,2,1:T(4,128)S(1)}, f32[6,3,3]{0,2,1:T(4,128)}, u32[]{:S(2)}) copy-start(f32[6,3,3]{0,2,1:T(4,128)} %param.10) | copy-start | bytes 652
  7.2 151.0 %all-gather.3.cloned.1.call-start = ((), (), s32[]{:S(2)}) async-start(), calls=%async_computation.2 | async-start | bytes 2297856 | tf_op jit(solution)/shard_map/all_gather | solution.py:172
  7.9 153.6 %all-gather.5.cloned.1.call-start = ((), (), s32[]{:S(2)}) async-start(), calls=%async_computation.3 | async-start | bytes 9191424 | tf_op jit(solution)/shard_map/all_gather | solution.py:178
  8.7 254.9 %reduce-scatter.3.cloned.1.call-start = ((), (), s32[]{:S(2)}) async-start(), calls=%async_computation.4 | async-start | bytes 4595712 | tf_op jit(solution)/shard_map/reduce_scatter | solution.py:195
  11.1 18.3 %collective-permute-start.1 = (f32[2,4,128,128]{3,2,1,0:T(8,128)S(1)}, f32[2,4,128,128]{3,2,1,0:T(8,128)S(1)}, u32[]{:S(2)}, u32[]{:S(2)}) collective-permute-start(f32[2,4,128,128]{3,2,1,0:T(8,128)S(1)} %get-tuple-element.32), channel_id=1, source_target_pairs={{2,0},{4,2},{6,4},{8,6},{10,8},{12,10},{14,12},{3,1},{5,3},{7,5},{... | collective-permute-start | bytes 1572872 | tf_op jit(solution)/shard_map/ppermute | solution.py:35
  12.4 28.4 %collective-permute-start = (f32[2,4,128,128]{3,2,1,0:T(8,128)S(1)}, f32[2,4,128,128]{3,2,1,0:T(8,128)S(1)}, u32[]{:S(2)}, u32[]{:S(2)}) collective-permute-start(f32[2,4,128,128]{3,2,1,0:T(8,128)S(1)} %get-tuple-element.31), channel_id=1, source_target_pairs={{0,2},{2,4},{4,6},{6,8},{8,10},{10,12},{12,14},{1,3},{3,5},{5,7},{... | collective-permute-start | bytes 1572872 | tf_op jit(solution)/shard_map/ppermute | solution.py:34
  81.3 6.9 %copy-start = (f32[1,16,128,128]{3,2,1,0:T(8,128)}, f32[1,16,128,128]{3,2,1,0:T(8,128)S(1)}, u32[]{:S(2)}) copy-start(f32[1,16,128,128]{3,2,1,0:T(8,128)S(1)} %select_bitcast_fusion) | copy-start | bytes 3145732
  84.7 3.5 copy-start.2
  88.2 1.1 copy-start.4
  89.4 9.0 %collective-permute-start.2 = (bf16[3,8,1,16,128]{4,3,2,1,0:T(8,128)(2,1)S(1)}, bf16[3,8,1,16,128]{4,3,2,1,0:T(8,128)(2,1)S(1)}, u32[]{:S(2)}, u32[]{:S(2)}) collective-permute-start(bf16[3,8,1,16,128]{4,3,2,1,0:T(8,128)(2,1)S(1)} %get-tuple-element.39), channel_id=1, source_target_pairs={{0,14},{2,0},{4,2},{6,4},{8,6},{10,8},{12,10},{14,12},{1,15},{3,1}... | collective-permute-start | bytes 294920 | tf_op jit(solution)/shard_map/ppermute | solution.py:22
  92.1 8.2 %collective-permute-start.3 = (bf16[3,8,1,16,128]{4,3,2,1,0:T(8,128)(2,1)S(1)}, bf16[3,8,1,16,128]{4,3,2,1,0:T(8,128)(2,1)S(1)}, u32[]{:S(2)}, u32[]{:S(2)}) collective-permute-start(bf16[3,8,1,16,128]{4,3,2,1,0:T(8,128)(2,1)S(1)} %get-tuple-element.38), channel_id=1, source_target_pairs={{0,12},{2,14},{4,0},{6,2},{8,4},{10,6},{12,8},{14,10},{1,13},{3,15... | collective-permute-start | bytes 294920 | tf_op jit(solution)/shard_map/ppermute | solution.py:22
  95.4 6.4 %collective-permute-start.4 = (bf16[3,8,1,16,128]{4,3,2,1,0:T(8,128)(2,1)S(1)}, bf16[3,8,1,16,128]{4,3,2,1,0:T(8,128)(2,1)S(1)}, u32[]{:S(2)}, u32[]{:S(2)}) collective-permute-start(bf16[3,8,1,16,128]{4,3,2,1,0:T(8,128)(2,1)S(1)} %get-tuple-element.37), channel_id=1, source_target_pairs={{0,10},{2,12},{4,14},{6,0},{8,2},{10,4},{12,6},{14,8},{1,11},{3,13... | collective-permute-start | bytes 294920 | tf_op jit(solution)/shard_map/ppermute | solution.py:22
  95.4 29.6 %collective-permute-start.5 = (bf16[3,8,1,16,128]{4,3,2,1,0:T(8,128)(2,1)S(1)}, bf16[3,8,1,16,128]{4,3,2,1,0:T(8,128)(2,1)S(1)}, u32[]{:S(2)}, u32[]{:S(2)}) collective-permute-start(bf16[3,8,1,16,128]{4,3,2,1,0:T(8,128)(2,1)S(1)} %get-tuple-element.36), channel_id=1, source_target_pairs={{0,8},{2,10},{4,12},{6,14},{8,0},{10,2},{12,4},{14,6},{1,9},{3,11}... | collective-permute-start | bytes 294920 | tf_op jit(solution)/shard_map/ppermute | solution.py:22
  97.5 28.3 %collective-permute-start.6 = (bf16[3,8,1,16,128]{4,3,2,1,0:T(8,128)(2,1)S(1)}, bf16[3,8,1,16,128]{4,3,2,1,0:T(8,128)(2,1)S(1)}, u32[]{:S(2)}, u32[]{:S(2)}) collective-permute-start(bf16[3,8,1,16,128]{4,3,2,1,0:T(8,128)(2,1)S(1)} %get-tuple-element.35), channel_id=1, source_target_pairs={{0,6},{2,8},{4,10},{6,12},{8,14},{10,0},{12,2},{14,4},{1,7},{3,9},... | collective-permute-start | bytes 294920 | tf_op jit(solution)/shard_map/ppermute | solution.py:22
  98.4 27.5 %collective-permute-start.7 = (bf16[3,8,1,16,128]{4,3,2,1,0:T(8,128)(2,1)S(1)}, bf16[3,8,1,16,128]{4,3,2,1,0:T(8,128)(2,1)S(1)}, u32[]{:S(2)}, u32[]{:S(2)}) collective-permute-start(bf16[3,8,1,16,128]{4,3,2,1,0:T(8,128)(2,1)S(1)} %get-tuple-element.34), channel_id=1, source_target_pairs={{0,4},{2,6},{4,8},{6,10},{8,12},{10,14},{12,0},{14,2},{1,5},{3,7},... | collective-permute-start | bytes 294920 | tf_op jit(solution)/shard_map/ppermute | solution.py:22
  100.3 25.6 %collective-permute-start.8 = (bf16[3,8,1,16,128]{4,3,2,1,0:T(8,128)(2,1)S(1)}, bf16[3,8,1,16,128]{4,3,2,1,0:T(8,128)(2,1)S(1)}, u32[]{:S(2)}, u32[]{:S(2)}) collective-permute-start(bf16[3,8,1,16,128]{4,3,2,1,0:T(8,128)(2,1)S(1)} %get-tuple-element.33), channel_id=1, source_target_pairs={{0,2},{2,4},{4,6},{6,8},{8,10},{10,12},{12,14},{14,0},{1,3},{3,5},... | collective-permute-start | bytes 294920 | tf_op jit(solution)/shard_map/ppermute | solution.py:22
  161.6 12.3 %copy-start.8 = (bf16[3072,1408]{1,0:T(8,128)(2,1)S(1)}, bf16[3072,1408]{1,0:T(8,128)(2,1)}, u32[]{:S(2)}) copy-start(bf16[3072,1408]{1,0:T(8,128)(2,1)} %all-gather.5.cloned.1.call-done) | copy-start | bytes 25952260
  173.8 5.1 %copy-start.9 = (bf16[512,3072]{1,0:T(8,128)(2,1)}, bf16[512,3072]{1,0:T(8,128)(2,1)S(1)}, u32[]{:S(2)}) copy-start(bf16[512,3072]{1,0:T(8,128)(2,1)S(1)} %fusion.2) | copy-start | bytes 9437188
  173.8 5.1 %copy-start.6 = (bf16[512,768]{0,1:T(8,128)(2,1)S(1)}, bf16[512,768]{0,1:T(8,128)(2,1)}, u32[]{:S(2)}) copy-start(bf16[512,768]{0,1:T(8,128)(2,1)} %reshape.61) | copy-start | bytes 2359300
  182.7 265.8 %reduce-scatter.5.cloned.1.call-start = ((), (), s32[]{:S(2)}) async-start(), calls=%async_computation.5 | async-start | bytes 18382848 | tf_op jit(solution)/shard_map/reduce_scatter | solution.py:183
  193.4 1.2 copy-start.1
  193.4 1.5 copy-start.3
  193.4 1.9 copy-start.5
Sparse Core Ops, SparseCore 0:
  10.2 54.4 all-gather.2
  67.0 81.9 all-gather.4
  182.8 80.6 reduce-scatter.2
  267.5 180.9 reduce-scatter.4
